TPU v7x, 512 devices: a whole 4x8x8 slice. The times are simulated.
512 devices in a mesh: seq: 32 (over y, x), trow: 2 (over core), tcol: 8 (over z).
Axes of the slice: x: 4, y: 8, z: 8, core: 2. Of those that a mesh axis runs over, the one named last changes fastest.
Arguments:
- tokens: bfloat16 [16384, 4096], P('seq', ('trow', 'tcol')), may hold values from -24 to 24
- norm_gain: float32 [4096], replicated, may hold values from 0.1 to 1.9
- in_weight: bfloat16 [3, 4096, 8192], P(None, None, ('trow', 'tcol')), may hold values from -0.09375 to 0.09375
- filter_taps: float32 [128, 8192], P(None, ('trow', 'tcol')), may hold values from -0.5 to 0.5
- conv_skip: float32 [8192], P(('trow', 'tcol')), may hold values from -1 to 1
- out_weight: bfloat16 [8192, 4096], P(('trow', 'tcol')), may hold values from -0.09375 to 0.09375
Outputs:
- mixer_out: bfloat16 [16384, 4096], P('seq', ('trow', 'tcol'))
All inputs are finite; a program needn't handle non-finite values.
Results may differ from a plain program's by a relative error of at most 0.03.
Values may be sent and summed in bfloat16 or wider, within the bound.
A program may use at most 64 MiB of HBM per device.

v0:
```python
import jax
import jax.numpy as jnp
from jax import lax
from jax.sharding import PartitionSpec as P


def passed_along(block, axis, distance):
    devices = range(lax.axis_size(axis))
    route = [(i - distance, i) for i in devices if i - distance in devices]
    return lax.ppermute(block, axis, route)


def on_device(tokens, norm_gain, in_weight, filter_taps, conv_skip, out_weight):
    whole = lax.all_gather(tokens, ("trow", "tcol"), axis=1, tiled=True)
    wide = whole.astype(jnp.float32)
    mean_square = jnp.mean(wide * wide, axis=1, keepdims=True)
    normed = (wide * lax.rsqrt(mean_square + 1e-06) * norm_gain).astype(jnp.bfloat16)
    query = jnp.dot(normed, in_weight[0], preferred_element_type=jnp.float32).astype(jnp.bfloat16)
    keys = jnp.dot(normed, in_weight[1], preferred_element_type=jnp.float32).astype(jnp.bfloat16)
    values = jnp.dot(normed, in_weight[2], preferred_element_type=jnp.float32).astype(jnp.bfloat16)
    mixed = (keys.astype(jnp.float32) * values.astype(jnp.float32)).astype(jnp.bfloat16)
    taps = filter_taps.shape[0]
    rows = mixed.shape[0]
    channels = mixed.shape[1]
    tail_rows = mixed[rows - (taps - 1) :]
    previous = passed_along(tail_rows, "seq", 1)
    extended = jnp.concatenate([previous, mixed], axis=0)

    def tap_group(group, total):
        for inner in range(8):
            index = group * 8 + inner
            window = lax.dynamic_slice_in_dim(extended, taps - 1 - index, rows, 0)
            weight = lax.dynamic_slice_in_dim(filter_taps, index, 1, 0)
            total = total + window.astype(jnp.float32) * weight
        return total

    filtered = lax.fori_loop(0, taps // 8, tap_group, jnp.zeros((rows, channels), jnp.float32))
    filtered = filtered + conv_skip * mixed.astype(jnp.float32)
    gated = (query.astype(jnp.float32) * filtered).astype(jnp.bfloat16)
    partial_sum = jnp.dot(gated, out_weight, preferred_element_type=jnp.float32)
    summed = lax.psum_scatter(
        partial_sum.astype(jnp.bfloat16), ("trow", "tcol"), scatter_dimension=1, tiled=True
    )
    return summed


def solution(mesh):
    placed = (
        P("seq", ("trow", "tcol")),
        P(),
        P(None, None, ("trow", "tcol")),
        P(None, ("trow", "tcol")),
        P(("trow", "tcol")),
        P(("trow", "tcol"), None),
    )
    return jax.shard_map(
        on_device, mesh=mesh, in_specs=placed, out_specs=P("seq", ("trow", "tcol")), check_vma=False
    )
```

profile of v0, /device:TPU:1, one launch (start us, length us, event | category | flops | bytes accessed | tf_op | source)
XLA Modules:
  0.0 220.7 jit_solution(7478278523960679927)
XLA Ops:
  6.5 0.0 all-gather.2.cloned.1.call-start
  6.5 0.7 all-gather.2.cloned.1.call-update
  7.3 0.0 reduce-scatter.2.cloned.1.call-start
  7.3 59.9 %all-gather.2.cloned.1.call-done = bf16[512,4096]{1,0:T(8,128)(2,1)} async-done(((bf16[512,256]{1,0:T(8,128)(2,1)}), bf16[512,4096]{1,0:T(8,128)(2,1)}) %all-gather.2.cloned.1.call-update) | async-done | bytes 4194320 | tf_op jit(solution)/shard_map/all_gather | solution.py:14
  67.2 3.2 %fusion.7 = f32[512]{0:T(512)S(1)} fusion(bf16[512,4096]{1,0:T(8,128)(2,1)} %all-gather.2.cloned.1.call-done), kind=kLoop, calls=%fused_computation.18 | loop fusion | flops 6290944 | bytes 4196352 | tf_op jit(solution)/shard_map/reduce_sum | solution.py:16
  70.4 0.2 copy-done
  70.6 4.6 %fusion.46 = f32[512,512]{1,0:T(8,128)S(1)} fusion(bf16[3,4096,512]{2,1,0:T(8,128)(2,1)} %param.10, bf16[512,4096]{1,0:T(8,128)(2,1)S(1)} %copy-done, f32[4096]{0:T(1024)S(1)} %copy-done.1, f32[512]{0:T(512)S(1)} %add_rsqrt_fusion), kind=kOutput, calls=%fused_computation.40 | convolution fusion | flops 2156396544 | bytes 9455616 | tf_op jit(solution)/shard_map/dot_general | solution.py:20
  75.2 4.6 %fusion.40 = bf16[512,512]{1,0:T(8,128)(2,1)S(1)} fusion(f32[512,512]{1,0:T(8,128)S(1)} %fusion.46, bf16[3,4096,512]{2,1,0:T(8,128)(2,1)} %param.10, bf16[512,4096]{1,0:T(8,128)(2,1)S(1)} %copy-done, f32[4096]{0:T(1024)S(1)} %copy-done.1, f32[512]{0:T(512)S(1)} %add_rsqrt_fusion), kind=kOutput, calls=%fused_computation.38 | convolution fusion | flops 2156920832 | bytes 9979904 | tf_op jit(solution)/shard_map/dot_general | solution.py:19
  79.8 3.1 %collective-permute-start = (bf16[127,512]{1,0:T(8,128)(2,1)S(1)}, bf16[127,512]{1,0:T(8,128)(2,1)S(1)}, u32[]{:S(2)}, u32[]{:S(2)}) collective-permute-start(bf16[127,512]{1,0:T(8,128)(2,1)S(1)} %slice.16), channel_id=1, source_target_pairs={{0,16},{16,32},{32,48},{48,64},{64,80},{80,96},{96,112},{112,128},... | collective-permute-start | bytes 390152 | tf_op jit(solution)/shard_map/ppermute | solution.py:10
  82.9 2.6 %collective-permute-done = bf16[127,512]{1,0:T(8,128)(2,1)S(1)} collective-permute-done((bf16[127,512]{1,0:T(8,128)(2,1)S(1)}, bf16[127,512]{1,0:T(8,128)(2,1)S(1)}, u32[]{:S(2)}, u32[]{:S(2)}) %collective-permute-start) | collective-permute-done | bytes 130080 | tf_op jit(solution)/shard_map/ppermute | solution.py:10
  85.5 0.1 pad_maximum_fusion
  85.6 0.0 copy-start.2
  85.6 39.9 %while.17 = (s32[]{:T(128)}, f32[512,512]{1,0:T(8,128)S(1)}, bf16[639,512]{1,0:T(8,128)(2,1)S(1)}, f32[128,512]{1,0:T(8,128)}, s32[]{:T(128)}, /*index=5*/s32[]{...) while((s32[]{:T(128)}, f32[512,512]{1,0:T(8,128)S(1)}, ...), condition=%wide.region_2.0_spmd.clone, body=%wide.region_1.0_spmd.clone.sunk | while | flops 6553667 | bytes 6341631 | solution.py:37
  85.7 1.0 constant_dynamic-slice_fusion.9
  86.8 1.4 fusion.58
  88.2 1.0 constant_dynamic-slice_fusion.9
  89.3 1.3 fusion.58
  90.7 1.0 constant_dynamic-slice_fusion.9
  91.8 1.4 fusion.58
  93.2 1.0 constant_dynamic-slice_fusion.9
  94.3 1.3 fusion.58
  95.7 1.0 constant_dynamic-slice_fusion.9
  96.8 1.4 fusion.58
  98.2 1.0 constant_dynamic-slice_fusion.9
  99.2 1.3 fusion.58
  100.7 1.0 constant_dynamic-slice_fusion.9
  101.7 1.4 fusion.58
  103.2 1.0 constant_dynamic-slice_fusion.9
  104.2 1.3 fusion.58
  105.7 1.0 constant_dynamic-slice_fusion.9
  106.7 1.4 fusion.58
  108.2 1.0 constant_dynamic-slice_fusion.9
  109.2 1.3 fusion.58
  110.7 1.0 constant_dynamic-slice_fusion.9
  111.7 1.4 fusion.58
  113.2 1.0 constant_dynamic-slice_fusion.9
  114.2 1.3 fusion.58
  115.7 1.0 constant_dynamic-slice_fusion.9
  116.7 1.4 fusion.58
  118.1 1.0 constant_dynamic-slice_fusion.9
  119.2 1.3 fusion.58
  120.6 1.0 constant_dynamic-slice_fusion.9
  121.7 1.4 fusion.58
  123.1 1.0 constant_dynamic-slice_fusion.9
  124.2 1.3 fusion.58
  125.5 11.2 %convolution_convert_fusion = bf16[512,4096]{1,0:T(8,128)(2,1)} fusion(bf16[512,4096]{1,0:T(8,128)(2,1)} %param.13, bf16[3,4096,512]{2,1,0:T(8,128)(2,1)} %param.10, f32[512,512]{1,0:T(8,128)S(1)} %get-tuple-element.156, bf16[512,512]{1,0:T(8,128)(2,1)S(1)} %fusion.40, f32[512]{0:T(512)S(1)} %copy-done.2, ...), kind=kOutput, calls=%fused_computation.21 | convolution fusion | flops 4307288064 | bytes 18370560 | tf_op jit(solution)/shard_map/dot_general | solution.py:40
  136.8 0.0 reduce-scatter.2.cloned.1.call-update
  136.8 77.0 %reduce-scatter.2.cloned.1.call-done = bf16[512,256]{1,0:T(8,128)(2,1)} async-done(((bf16[512,4096]{1,0:T(8,128)(2,1)}), bf16[512,256]{1,0:T(8,128)(2,1)}) %reduce-scatter.2.cloned.1.call-update) | async-done | bytes 262160 | tf_op jit(solution)/shard_map/reduce_scatter | solution.py:41
  (7 shorter events, 0.1 us)
Async XLA Ops:
  6.5 63.9 %copy-start.1 = (f32[4096]{0:T(1024)S(1)}, f32[4096]{0:T(1024)}, u32[]{:S(2)}) copy-start(f32[4096]{0:T(1024)} %param.9) | copy-start | bytes 49156
  6.5 60.6 %all-gather.2.cloned.1.call-start = ((), (), s32[]{:S(2)}) async-start(), calls=%async_computation.1 | async-start | bytes 4456448 | tf_op jit(solution)/shard_map/all_gather | solution.py:14
  7.3 206.6 %reduce-scatter.2.cloned.1.call-start = ((), (), s32[]{:S(2)}) async-start(), calls=%async_computation.2 | async-start | bytes 4456448 | tf_op jit(solution)/shard_map/reduce_scatter | solution.py:41
  67.2 3.4 %copy-start = (bf16[512,4096]{1,0:T(8,128)(2,1)S(1)}, bf16[512,4096]{1,0:T(8,128)(2,1)}, u32[]{:S(2)}) copy-start(bf16[512,4096]{1,0:T(8,128)(2,1)} %all-gather.2.cloned.1.call-done) | copy-start | bytes 12582916
  79.8 5.7 %collective-permute-start = (bf16[127,512]{1,0:T(8,128)(2,1)S(1)}, bf16[127,512]{1,0:T(8,128)(2,1)S(1)}, u32[]{:S(2)}, u32[]{:S(2)}) collective-permute-start(bf16[127,512]{1,0:T(8,128)(2,1)S(1)} %slice.16), channel_id=1, source_target_pairs={{0,16},{16,32},{32,48},{48,64},{64,80},{80,96},{96,112},{112,128},... | collective-permute-start | bytes 390152 | tf_op jit(solution)/shard_map/ppermute | solution.py:10
  85.6 39.9 %copy-start.2 = (f32[512]{0:T(512)S(1)}, f32[512]{0:T(512)}, u32[]{:S(2)}) copy-start(f32[512]{0:T(512)} %param.12) | copy-start | bytes 6148
Sparse Core Ops, SparseCore 0:
  9.4 57.7 all-gather.1
  136.9 76.8 reduce-scatter.1
where the time goes:
time: 222 us; the launch traced here: 221 us
  waiting for transfers between devices  140 us (63%)
  other arithmetic  25 us (11%)
  matrix products  20.4 us (9%)
  local copies, waits for them, and re-layouts  16.9 us (8%)
  between operations  13.5 us (6%)
  starting transfers between devices  3.13 us (1%)
    reduce_scatter x1, waiting for transfers between devices, on_device(): lax.psum_scatter(partial_sum.astype(jnp.bfloat16), ('trow', 'tcol'), scat...  77 us
    all_gather x1, waiting for transfers between devices, on_device(): whole = lax.all_gather(tokens, ('trow', 'tcol'), axis=1, tiled=True)  59.9 us
    add x16, other arithmetic, tap_group(): total = total + window.astype(jnp.float32) * weight  21.6 us
    dynamic_slice x16, local copies, waits for them, and re-layouts, tap_group(): weight = lax.dynamic_slice_in_dim(filter_taps, index, 1, 0)  16.6 us
    dot_general x1, matrix products, on_device(): partial_sum = jnp.dot(gated, out_weight, preferred_element_type=jnp.float32)  11.2 us
    dot_general x1, matrix products, on_device(): jnp.dot(normed, in_weight[1], preferred_element_type=jnp.float32)  4.58 us
    dot_general x1, matrix products, on_device(): jnp.dot(normed, in_weight[2], preferred_element_type=jnp.float32)  4.56 us
  transfers between devices with their start and end apart: 3, of which 3 were waited for; matrix products, arithmetic and copies ran while one was open for 0% of the time, Pallas kernels for 0%

commit v1 on v0

--- a/solution.py
+++ b/solution.py
@@ -11,7 +11,27 @@
 
 
 def on_device(tokens, norm_gain, in_weight, filter_taps, conv_skip, out_weight):
-    whole = lax.all_gather(tokens, ("trow", "tcol"), axis=1, tiled=True)
+    size, here, span = (
+        lax.axis_size(("trow", "tcol")),
+        lax.axis_index(("trow", "tcol")),
+        tokens.shape[1],
+    )
+    ahead = [(i_2, (i_2 + 1) % size) for i_2 in range(size)]
+    behind = [(i_2, (i_2 - 1) % size) for i_2 in range(size)]
+    whole = jnp.zeros((*tokens.shape[:1], size * span, *tokens.shape[1 + 1 :]), tokens.dtype)
+    whole = lax.dynamic_update_slice_in_dim(whole, tokens, here * span, axis=1)
+    from_left = from_right = tokens
+    middle = size // 2
+    for step in range(1, middle + 1):
+        from_left = lax.ppermute(from_left, ("trow", "tcol"), ahead)
+        whole = lax.dynamic_update_slice_in_dim(
+            whole, from_left, (here - step) % size * span, axis=1
+        )
+        if step < size - middle:
+            from_right = lax.ppermute(from_right, ("trow", "tcol"), behind)
+            whole = lax.dynamic_update_slice_in_dim(
+                whole, from_right, (here + step) % size * span, axis=1
+            )
     wide = whole.astype(jnp.float32)
     mean_square = jnp.mean(wide * wide, axis=1, keepdims=True)
     normed = (wide * lax.rsqrt(mean_square + 1e-06) * norm_gain).astype(jnp.bfloat16)

time: 222 us -> 261 us (1.18)
  starting transfers between devices: 3.13 us -> 63.4 us
  waiting for transfers between devices: 140 us -> 100 us
  local copies, waits for them, and re-layouts: 16.9 us -> 31.2 us
    ppermute x0 -> x15, starting transfers between devices: none -> 60.1 us  [the longest x7 41.8 us: on_device(): from_right = lax.ppermute(from_right, ('trow', 'tcol'), behind)]
    all_gather x1 -> x0, waiting for transfers between devices: 59.9 us -> none  [on_device(): whole = lax.all_gather(tokens, ('trow', 'tcol'), axis=1, tiled=True)]
    ppermute x0 -> x15, waiting for transfers between devices: none -> 23.2 us  [the longest x8 15.7 us: on_device(): from_left = lax.ppermute(from_left, ('trow', 'tcol'), ahead)]
    dynamic_update_slice x0 -> x16, local copies, waits for them, and re-layouts: none -> 12 us  [the longest x8 6.01 us: on_device(): lax.dynamic_update_slice_in_dim(whole, from_left, (here - step) % size *...]
    reduce_scatter x1, waiting for transfers between devices: 77 us -> 74.3 us  [on_device(): lax.psum_scatter(partial_sum.astype(jnp.bfloat16), ('trow', 'tcol'), scat...]
  transfers between devices with their start and end apart: 3 -> 17, of which waited for: 3 -> 12; matrix products, arithmetic and copies ran while one was open for 0% -> 5% of each run, Pallas kernels for 0% -> 0%
where the time goes in v1:
time: 261 us; the launch traced here: 259 us
  waiting for transfers between devices  100 us (38%)
  starting transfers between devices  63.4 us (24%)
  local copies, waits for them, and re-layouts  31.2 us (12%)
  other arithmetic  25.2 us (10%)
  matrix products  22.9 us (9%)
  between operations  13.6 us (5%)
    reduce_scatter x1, waiting for transfers between devices, on_device(): lax.psum_scatter(partial_sum.astype(jnp.bfloat16), ('trow', 'tcol'), scat...  74.3 us
    ppermute x7, starting transfers between devices, on_device(): from_right = lax.ppermute(from_right, ('trow', 'tcol'), behind)  41.8 us
    add x16, other arithmetic, tap_group(): total = total + window.astype(jnp.float32) * weight  21.9 us
    ppermute x8, starting transfers between devices, on_device(): from_left = lax.ppermute(from_left, ('trow', 'tcol'), ahead)  18.3 us
    dynamic_slice x16, local copies, waits for them, and re-layouts, tap_group(): weight = lax.dynamic_slice_in_dim(filter_taps, index, 1, 0)  16.6 us
    ppermute x8, waiting for transfers between devices, on_device(): from_left = lax.ppermute(from_left, ('trow', 'tcol'), ahead)  15.7 us
    dot_general x1, matrix products, on_device(): partial_sum = jnp.dot(gated, out_weight, preferred_element_type=jnp.float32)  11.2 us
    ppermute x7, waiting for transfers between devices, on_device(): from_right = lax.ppermute(from_right, ('trow', 'tcol'), behind)  7.56 us
  transfers between devices with their start and end apart: 17, of which 12 were waited for; matrix products, arithmetic and copies ran while one was open for 5% of the time, Pallas kernels for 0%

profile of v1, /device:TPU:1, one launch (start us, length us, event | category | flops | bytes accessed | tf_op | source)
XLA Modules:
  0.0 258.6 jit_solution(4573460136492094979)
XLA Ops:
  6.5 4.9 %collective-permute-start = (bf16[512,256]{1,0:T(8,128)(2,1)}, bf16[512,256]{1,0:T(8,128)(2,1)S(1)}, u32[]{:S(2)}, u32[]{:S(2)}) collective-permute-start(bf16[512,256]{1,0:T(8,128)(2,1)} %param.8), channel_id=1, source_target_pairs={{0,1},{1,2},{2,3},{3,4},{4,5},{5,6},{6,7},{7,8},{8,9},{9,10},{10,1... | collective-permute-start | bytes 786440 | tf_op jit(solution)/shard_map/ppermute | solution.py:26
  11.5 9.1 %collective-permute-start.1 = (bf16[512,256]{1,0:T(8,128)(2,1)}, bf16[512,256]{1,0:T(8,128)(2,1)S(1)}, u32[]{:S(2)}, u32[]{:S(2)}) collective-permute-start(bf16[512,256]{1,0:T(8,128)(2,1)} %param.8), channel_id=1, source_target_pairs={{0,15},{1,0},{2,1},{3,2},{4,3},{5,4},{6,5},{7,6},{8,7},{9,8},{10,9... | collective-permute-start | bytes 786440 | tf_op jit(solution)/shard_map/ppermute | solution.py:31
  20.7 4.3 %collective-permute-done = bf16[512,256]{1,0:T(8,128)(2,1)S(1)} collective-permute-done((bf16[512,256]{1,0:T(8,128)(2,1)}, bf16[512,256]{1,0:T(8,128)(2,1)S(1)}, u32[]{:S(2)}, u32[]{:S(2)}) %collective-permute-start) | collective-permute-done | bytes 262176 | tf_op jit(solution)/shard_map/ppermute | solution.py:26
  24.9 1.9 collective-permute-start.2
  27.1 5.5 %collective-permute-start.3 = (bf16[512,256]{1,0:T(8,128)(2,1)S(1)}, bf16[512,256]{1,0:T(8,128)(2,1)S(1)}, u32[]{:S(2)}, u32[]{:S(2)}) collective-permute-start(bf16[512,256]{1,0:T(8,128)(2,1)S(1)} %collective-permute-done.1), channel_id=1, source_target_pairs={{0,15},{1,0},{2,1},{3,2},{4,3},{5,4},{6,5},{7,6},{8,7},{9,8},{10,9... | collective-permute-start | bytes 786440 | tf_op jit(solution)/shard_map/ppermute | solution.py:31
  32.5 3.2 %collective-permute-done.2 = bf16[512,256]{1,0:T(8,128)(2,1)S(1)} collective-permute-done((bf16[512,256]{1,0:T(8,128)(2,1)S(1)}, bf16[512,256]{1,0:T(8,128)(2,1)S(1)}, u32[]{:S(2)}, u32[]{:S(2)}) %collective-permute-start.2) | collective-permute-done | bytes 262176 | tf_op jit(solution)/shard_map/ppermute | solution.py:26
  35.8 1.9 collective-permute-start.4
  38.4 5.6 %collective-permute-start.5 = (bf16[512,256]{1,0:T(8,128)(2,1)S(1)}, bf16[512,256]{1,0:T(8,128)(2,1)S(1)}, u32[]{:S(2)}, u32[]{:S(2)}) collective-permute-start(bf16[512,256]{1,0:T(8,128)(2,1)S(1)} %collective-permute-done.3), channel_id=1, source_target_pairs={{0,15},{1,0},{2,1},{3,2},{4,3},{5,4},{6,5},{7,6},{8,7},{9,8},{10,9... | collective-permute-start | bytes 786440 | tf_op jit(solution)/shard_map/ppermute | solution.py:31
  44.0 2.7 %collective-permute-done.4 = bf16[512,256]{1,0:T(8,128)(2,1)S(1)} collective-permute-done((bf16[512,256]{1,0:T(8,128)(2,1)S(1)}, bf16[512,256]{1,0:T(8,128)(2,1)S(1)}, u32[]{:S(2)}, u32[]{:S(2)}) %collective-permute-start.4) | collective-permute-done | bytes 262176 | tf_op jit(solution)/shard_map/ppermute | solution.py:26
  46.7 1.9 collective-permute-start.6
  48.6 2.5 broadcast_in_dim.4
  52.6 4.8 %collective-permute-start.7 = (bf16[512,256]{1,0:T(8,128)(2,1)S(1)}, bf16[512,256]{1,0:T(8,128)(2,1)S(1)}, u32[]{:S(2)}, u32[]{:S(2)}) collective-permute-start(bf16[512,256]{1,0:T(8,128)(2,1)S(1)} %collective-permute-done.5), channel_id=1, source_target_pairs={{0,15},{1,0},{2,1},{3,2},{4,3},{5,4},{6,5},{7,6},{8,7},{9,8},{10,9... | collective-permute-start | bytes 786440 | tf_op jit(solution)/shard_map/ppermute | solution.py:31
  58.2 1.9 collective-permute-start.8
  61.7 1.8 collective-permute-done.7
  63.5 5.6 %collective-permute-start.9 = (bf16[512,256]{1,0:T(8,128)(2,1)S(1)}, bf16[512,256]{1,0:T(8,128)(2,1)S(1)}, u32[]{:S(2)}, u32[]{:S(2)}) collective-permute-start(bf16[512,256]{1,0:T(8,128)(2,1)S(1)} %collective-permute-done.7), channel_id=1, source_target_pairs={{0,15},{1,0},{2,1},{3,2},{4,3},{5,4},{6,5},{7,6},{8,7},{9,8},{10,9... | collective-permute-start | bytes 786440 | tf_op jit(solution)/shard_map/ppermute | solution.py:31
  69.8 1.9 collective-permute-start.10
  73.3 1.6 collective-permute-done.9
  74.9 5.6 %collective-permute-start.11 = (bf16[512,256]{1,0:T(8,128)(2,1)S(1)}, bf16[512,256]{1,0:T(8,128)(2,1)S(1)}, u32[]{:S(2)}, u32[]{:S(2)}) collective-permute-start(bf16[512,256]{1,0:T(8,128)(2,1)S(1)} %collective-permute-done.9), channel_id=1, source_target_pairs={{0,15},{1,0},{2,1},{3,2},{4,3},{5,4},{6,5},{7,6},{8,7},{9,8},{10,9... | collective-permute-start | bytes 786440 | tf_op jit(solution)/shard_map/ppermute | solution.py:31
  81.3 1.9 collective-permute-start.12
  84.7 1.6 collective-permute-done.11
  86.3 5.6 %collective-permute-start.13 = (bf16[512,256]{1,0:T(8,128)(2,1)S(1)}, bf16[512,256]{1,0:T(8,128)(2,1)S(1)}, u32[]{:S(2)}, u32[]{:S(2)}) collective-permute-start(bf16[512,256]{1,0:T(8,128)(2,1)S(1)} %collective-permute-done.11), channel_id=1, source_target_pairs={{0,15},{1,0},{2,1},{3,2},{4,3},{5,4},{6,5},{7,6},{8,7},{9,8},{10,9... | collective-permute-start | bytes 786440 | tf_op jit(solution)/shard_map/ppermute | solution.py:31
  92.6 1.9 collective-permute-start.14
  96.0 1.7 collective-permute-done.13
  98.4 5.4 %collective-permute-done.14 = bf16[512,256]{1,0:T(8,128)(2,1)S(1)} collective-permute-done((bf16[512,256]{1,0:T(8,128)(2,1)S(1)}, bf16[512,256]{1,0:T(8,128)(2,1)S(1)}, u32[]{:S(2)}, u32[]{:S(2)}) %collective-permute-start.14) | collective-permute-done | bytes 262176 | tf_op jit(solution)/shard_map/ppermute | solution.py:26
  104.6 3.1 %fusion.7 = f32[512]{0:T(512)S(1)} fusion(bf16[512,4096]{1,0:T(8,128)(2,1)} %constant_dynamic-update-slice_fusion), kind=kLoop, calls=%fused_computation.18 | loop fusion | flops 6290944 | bytes 4196352 | tf_op jit(solution)/shard_map/reduce_sum | solution.py:36
  107.7 5.8 %fusion.46 = f32[512,512]{1,0:T(8,128)S(1)} fusion(bf16[3,4096,512]{2,1,0:T(8,128)(2,1)} %param.10, bf16[512,4096]{1,0:T(8,128)(2,1)} %constant_dynamic-update-slice_fusion, f32[4096]{0:T(1024)S(1)} %copy-done.1, f32[512]{0:T(512)S(1)} %add_rsqrt_fusion), kind=kOutput, calls=%fused_computation.40 | convolution fusion | flops 2156396544 | bytes 9455616 | tf_op jit(solution)/shard_map/dot_general | solution.py:40
  113.5 5.8 %fusion.40 = bf16[512,512]{1,0:T(8,128)(2,1)S(1)} fusion(f32[512,512]{1,0:T(8,128)S(1)} %fusion.46, bf16[3,4096,512]{2,1,0:T(8,128)(2,1)} %param.10, bf16[512,4096]{1,0:T(8,128)(2,1)} %constant_dynamic-update-slice_fusion, f32[4096]{0:T(1024)S(1)} %copy-done.1, f32[512]{0:T(512)S(1)} %add_rsqrt_fusion), kind=kOutput, calls=%fused_computation.38 | convolution fusion | flops 2156920832 | bytes 9979904 | tf_op jit(solution)/shard_map/dot_general | solution.py:39
  119.4 3.3 %collective-permute-start.15 = (bf16[127,512]{1,0:T(8,128)(2,1)S(1)}, bf16[127,512]{1,0:T(8,128)(2,1)S(1)}, u32[]{:S(2)}, u32[]{:S(2)}) collective-permute-start(bf16[127,512]{1,0:T(8,128)(2,1)S(1)} %slice.16), channel_id=1, source_target_pairs={{0,16},{16,32},{32,48},{48,64},{64,80},{80,96},{96,112},{112,128},... | collective-permute-start | bytes 390152 | tf_op jit(solution)/shard_map/ppermute | solution.py:10
  122.7 2.4 collective-permute-done.15
  125.3 40.9 %while.17 = (s32[]{:T(128)}, f32[512,512]{1,0:T(8,128)S(1)}, bf16[639,512]{1,0:T(8,128)(2,1)S(1)}, f32[128,512]{1,0:T(8,128)}, s32[]{:T(128)}, /*index=5*/s32[]{...) while((s32[]{:T(128)}, f32[512,512]{1,0:T(8,128)S(1)}, ...), condition=%wide.region_2.3_spmd.clone, body=%wide.region_1.2_spmd.clone.sunk | while | flops 6553667 | bytes 6341623 | solution.py:57
  126.5 1.4 fusion.58
  129.0 1.4 fusion.58
  131.6 1.4 fusion.58
  134.1 1.4 fusion.58
  136.7 1.4 fusion.58
  139.3 1.4 fusion.58
  141.8 1.4 fusion.58
  144.4 1.4 fusion.58
  146.9 1.4 fusion.58
  149.5 1.4 fusion.58
  152.0 1.4 fusion.58
  154.6 1.4 fusion.58
  157.2 1.4 fusion.58
  159.7 1.4 fusion.58
  162.3 1.4 fusion.58
  164.8 1.4 fusion.58
  166.2 11.2 %convolution_convert_fusion = bf16[512,4096]{1,0:T(8,128)(2,1)} fusion(bf16[512,4096]{1,0:T(8,128)(2,1)} %param.13, bf16[3,4096,512]{2,1,0:T(8,128)(2,1)} %param.10, f32[512,512]{1,0:T(8,128)S(1)} %get-tuple-element.156, bf16[512,512]{1,0:T(8,128)(2,1)S(1)} %fusion.40, f32[512]{0:T(512)S(1)} %copy-done.2, ...), kind=kOutput, calls=%fused_computation.21 | convolution fusion | flops 4307288064 | bytes 18370560 | tf_op jit(solution)/shard_map/dot_general | solution.py:60
  177.5 74.3 %reduce-scatter.2.cloned.1.call-done = bf16[512,256]{1,0:T(8,128)(2,1)} async-done(((bf16[512,4096]{1,0:T(8,128)(2,1)}), bf16[512,256]{1,0:T(8,128)(2,1)}) %reduce-scatter.2.cloned.1.call-update) | async-done | bytes 262160 | tf_op jit(solution)/shard_map/reduce_scatter | solution.py:61
  (51 shorter events, 29.8 us)
Async XLA Ops:
  6.5 44.5 %copy-start = (bf16[512,256]{1,0:T(8,128)(2,1)S(1)}, bf16[512,256]{1,0:T(8,128)(2,1)}, u32[]{:S(2)}) copy-start(bf16[512,256]{1,0:T(8,128)(2,1)} %param.8) | copy-start | bytes 786436
  6.5 245.2 %reduce-scatter.2.cloned.1.call-start = ((), (), s32[]{:S(2)}) async-start(), calls=%async_computation.1 | async-start | bytes 4456448 | tf_op jit(solution)/shard_map/reduce_scatter | solution.py:61
  6.5 18.4 %collective-permute-start = (bf16[512,256]{1,0:T(8,128)(2,1)}, bf16[512,256]{1,0:T(8,128)(2,1)S(1)}, u32[]{:S(2)}, u32[]{:S(2)}) collective-permute-start(bf16[512,256]{1,0:T(8,128)(2,1)} %param.8), channel_id=1, source_target_pairs={{0,1},{1,2},{2,3},{3,4},{4,5},{5,6},{6,7},{7,8},{8,9},{9,10},{10,1... | collective-permute-start | bytes 786440 | tf_op jit(solution)/shard_map/ppermute | solution.py:26
  11.5 15.6 %collective-permute-start.1 = (bf16[512,256]{1,0:T(8,128)(2,1)}, bf16[512,256]{1,0:T(8,128)(2,1)S(1)}, u32[]{:S(2)}, u32[]{:S(2)}) collective-permute-start(bf16[512,256]{1,0:T(8,128)(2,1)} %param.8), channel_id=1, source_target_pairs={{0,15},{1,0},{2,1},{3,2},{4,3},{5,4},{6,5},{7,6},{8,7},{9,8},{10,9... | collective-permute-start | bytes 786440 | tf_op jit(solution)/shard_map/ppermute | solution.py:31
  24.9 10.9 %collective-permute-start.2 = (bf16[512,256]{1,0:T(8,128)(2,1)S(1)}, bf16[512,256]{1,0:T(8,128)(2,1)S(1)}, u32[]{:S(2)}, u32[]{:S(2)}) collective-permute-start(bf16[512,256]{1,0:T(8,128)(2,1)S(1)} %collective-permute-done), channel_id=1, source_target_pairs={{0,1},{1,2},{2,3},{3,4},{4,5},{5,6},{6,7},{7,8},{8,9},{9,10},{10,1... | collective-permute-start | bytes 786440 | tf_op jit(solution)/shard_map/ppermute | solution.py:26
  27.1 11.3 %collective-permute-start.3 = (bf16[512,256]{1,0:T(8,128)(2,1)S(1)}, bf16[512,256]{1,0:T(8,128)(2,1)S(1)}, u32[]{:S(2)}, u32[]{:S(2)}) collective-permute-start(bf16[512,256]{1,0:T(8,128)(2,1)S(1)} %collective-permute-done.1), channel_id=1, source_target_pairs={{0,15},{1,0},{2,1},{3,2},{4,3},{5,4},{6,5},{7,6},{8,7},{9,8},{10,9... | collective-permute-start | bytes 786440 | tf_op jit(solution)/shard_map/ppermute | solution.py:31
  35.8 10.9 %collective-permute-start.4 = (bf16[512,256]{1,0:T(8,128)(2,1)S(1)}, bf16[512,256]{1,0:T(8,128)(2,1)S(1)}, u32[]{:S(2)}, u32[]{:S(2)}) collective-permute-start(bf16[512,256]{1,0:T(8,128)(2,1)S(1)} %collective-permute-done.2), channel_id=1, source_target_pairs={{0,1},{1,2},{2,3},{3,4},{4,5},{5,6},{6,7},{7,8},{8,9},{9,10},{10,1... | collective-permute-start | bytes 786440 | tf_op jit(solution)/shard_map/ppermute | solution.py:26
  38.4 14.2 %collective-permute-start.5 = (bf16[512,256]{1,0:T(8,128)(2,1)S(1)}, bf16[512,256]{1,0:T(8,128)(2,1)S(1)}, u32[]{:S(2)}, u32[]{:S(2)}) collective-permute-start(bf16[512,256]{1,0:T(8,128)(2,1)S(1)} %collective-permute-done.3), channel_id=1, source_target_pairs={{0,15},{1,0},{2,1},{3,2},{4,3},{5,4},{6,5},{7,6},{8,7},{9,8},{10,9... | collective-permute-start | bytes 786440 | tf_op jit(solution)/shard_map/ppermute | solution.py:31
  46.7 11.5 %collective-permute-start.6 = (bf16[512,256]{1,0:T(8,128)(2,1)S(1)}, bf16[512,256]{1,0:T(8,128)(2,1)S(1)}, u32[]{:S(2)}, u32[]{:S(2)}) collective-permute-start(bf16[512,256]{1,0:T(8,128)(2,1)S(1)} %collective-permute-done.4), channel_id=1, source_target_pairs={{0,1},{1,2},{2,3},{3,4},{4,5},{5,6},{6,7},{7,8},{8,9},{9,10},{10,1... | collective-permute-start | bytes 786440 | tf_op jit(solution)/shard_map/ppermute | solution.py:26
  52.6 10.9 %collective-permute-start.7 = (bf16[512,256]{1,0:T(8,128)(2,1)S(1)}, bf16[512,256]{1,0:T(8,128)(2,1)S(1)}, u32[]{:S(2)}, u32[]{:S(2)}) collective-permute-start(bf16[512,256]{1,0:T(8,128)(2,1)S(1)} %collective-permute-done.5), channel_id=1, source_target_pairs={{0,15},{1,0},{2,1},{3,2},{4,3},{5,4},{6,5},{7,6},{8,7},{9,8},{10,9... | collective-permute-start | bytes 786440 | tf_op jit(solution)/shard_map/ppermute | solution.py:31
  58.2 11.6 %collective-permute-start.8 = (bf16[512,256]{1,0:T(8,128)(2,1)S(1)}, bf16[512,256]{1,0:T(8,128)(2,1)S(1)}, u32[]{:S(2)}, u32[]{:S(2)}) collective-permute-start(bf16[512,256]{1,0:T(8,128)(2,1)S(1)} %collective-permute-done.6), channel_id=1, source_target_pairs={{0,1},{1,2},{2,3},{3,4},{4,5},{5,6},{6,7},{7,8},{8,9},{9,10},{10,1... | collective-permute-start | bytes 786440 | tf_op jit(solution)/shard_map/ppermute | solution.py:26
  63.5 11.4 %collective-permute-start.9 = (bf16[512,256]{1,0:T(8,128)(2,1)S(1)}, bf16[512,256]{1,0:T(8,128)(2,1)S(1)}, u32[]{:S(2)}, u32[]{:S(2)}) collective-permute-start(bf16[512,256]{1,0:T(8,128)(2,1)S(1)} %collective-permute-done.7), channel_id=1, source_target_pairs={{0,15},{1,0},{2,1},{3,2},{4,3},{5,4},{6,5},{7,6},{8,7},{9,8},{10,9... | collective-permute-start | bytes 786440 | tf_op jit(solution)/shard_map/ppermute | solution.py:31
  69.8 11.4 %collective-permute-start.10 = (bf16[512,256]{1,0:T(8,128)(2,1)S(1)}, bf16[512,256]{1,0:T(8,128)(2,1)S(1)}, u32[]{:S(2)}, u32[]{:S(2)}) collective-permute-start(bf16[512,256]{1,0:T(8,128)(2,1)S(1)} %collective-permute-done.8), channel_id=1, source_target_pairs={{0,1},{1,2},{2,3},{3,4},{4,5},{5,6},{6,7},{7,8},{8,9},{9,10},{10,1... | collective-permute-start | bytes 786440 | tf_op jit(solution)/shard_map/ppermute | solution.py:26
  73.3 34.4 %copy-start.1 = (f32[4096]{0:T(1024)S(1)}, f32[4096]{0:T(1024)}, u32[]{:S(2)}) copy-start(f32[4096]{0:T(1024)} %param.9) | copy-start | bytes 49156
  74.9 11.4 %collective-permute-start.11 = (bf16[512,256]{1,0:T(8,128)(2,1)S(1)}, bf16[512,256]{1,0:T(8,128)(2,1)S(1)}, u32[]{:S(2)}, u32[]{:S(2)}) collective-permute-start(bf16[512,256]{1,0:T(8,128)(2,1)S(1)} %collective-permute-done.9), channel_id=1, source_target_pairs={{0,15},{1,0},{2,1},{3,2},{4,3},{5,4},{6,5},{7,6},{8,7},{9,8},{10,9... | collective-permute-start | bytes 786440 | tf_op jit(solution)/shard_map/ppermute | solution.py:31
  81.3 11.4 %collective-permute-start.12 = (bf16[512,256]{1,0:T(8,128)(2,1)S(1)}, bf16[512,256]{1,0:T(8,128)(2,1)S(1)}, u32[]{:S(2)}, u32[]{:S(2)}) collective-permute-start(bf16[512,256]{1,0:T(8,128)(2,1)S(1)} %collective-permute-done.10), channel_id=1, source_target_pairs={{0,1},{1,2},{2,3},{3,4},{4,5},{5,6},{6,7},{7,8},{8,9},{9,10},{10,1... | collective-permute-start | bytes 786440 | tf_op jit(solution)/shard_map/ppermute | solution.py:26
  86.3 11.4 %collective-permute-start.13 = (bf16[512,256]{1,0:T(8,128)(2,1)S(1)}, bf16[512,256]{1,0:T(8,128)(2,1)S(1)}, u32[]{:S(2)}, u32[]{:S(2)}) collective-permute-start(bf16[512,256]{1,0:T(8,128)(2,1)S(1)} %collective-permute-done.11), channel_id=1, source_target_pairs={{0,15},{1,0},{2,1},{3,2},{4,3},{5,4},{6,5},{7,6},{8,7},{9,8},{10,9... | collective-permute-start | bytes 786440 | tf_op jit(solution)/shard_map/ppermute | solution.py:31
  92.6 11.2 %collective-permute-start.14 = (bf16[512,256]{1,0:T(8,128)(2,1)S(1)}, bf16[512,256]{1,0:T(8,128)(2,1)S(1)}, u32[]{:S(2)}, u32[]{:S(2)}) collective-permute-start(bf16[512,256]{1,0:T(8,128)(2,1)S(1)} %collective-permute-done.12), channel_id=1, source_target_pairs={{0,1},{1,2},{2,3},{3,4},{4,5},{5,6},{6,7},{7,8},{8,9},{9,10},{10,1... | collective-permute-start | bytes 786440 | tf_op jit(solution)/shard_map/ppermute | solution.py:26
  119.4 5.7 %collective-permute-start.15 = (bf16[127,512]{1,0:T(8,128)(2,1)S(1)}, bf16[127,512]{1,0:T(8,128)(2,1)S(1)}, u32[]{:S(2)}, u32[]{:S(2)}) collective-permute-start(bf16[127,512]{1,0:T(8,128)(2,1)S(1)} %slice.16), channel_id=1, source_target_pairs={{0,16},{16,32},{32,48},{48,64},{64,80},{80,96},{96,112},{112,128},... | collective-permute-start | bytes 390152 | tf_op jit(solution)/shard_map/ppermute | solution.py:10
  125.3 40.9 %copy-start.2 = (f32[512]{0:T(512)S(1)}, f32[512]{0:T(512)}, u32[]{:S(2)}) copy-start(f32[512]{0:T(512)} %param.12) | copy-start | bytes 6148
Sparse Core Ops, SparseCore 0:
  177.6 74.1 reduce-scatter.1
